TPU v7x, 128 devices: a whole 4x4x4 slice. The times are simulated.
128 devices in a mesh: row: 8 (over z, core), col: 16 (over x, y).
Axes of the slice: x: 4, y: 4, z: 4, core: 2. Of those that a mesh axis runs over, the one named last changes fastest.
Arguments:
- block_values: bfloat16 [8, 16, 256, 128, 128], P('row', 'col'), may hold values from -1.2 to 1.2
- block_rows: int32 [8, 16, 256], P('row', 'col'), may hold values from 0 to 207, as said below
- block_cols: int32 [8, 16, 256], P('row', 'col'), may hold values from 0 to 103, as said below
- start_vectors: bfloat16 [212992, 256], P(('row', 'col')), may hold values from -6 to 6
- center: float32 [1], replicated, may hold values from -0.5 to -0.1
- half_width: float32 [1], replicated, may hold values from 0.9 to 1.3
- row_counts: int32 [128], replicated, may hold values from 7 to 19, as said below
Outputs:
- relaid: bfloat16 [311296, 256], P(('row', 'col'))
Inputs may be any that keep to these rules, and one draw needn't show every extreme that they name: `block_rows`: the first 13 entries of cell (r, c) are its diagonal blocks, at local row c * 13 + k; the rest are anywhere; positions may repeat, and repeated blocks add. `block_cols`: the first 13 entries of cell (r, c) are at local column r * 13 + k. `row_counts`: entries 2 i and 2 i + 1 sum to 26; entry 0 is larger than 13.
All inputs are finite; a program needn't handle non-finite values.
Results may differ from a plain program's by a relative error of at most 0.019.
Values may be sent and summed in bfloat16 or wider, within the bound.
A program may use at most 192 MiB of HBM per device.

v0:
```python
import math
import jax
import jax.numpy as jnp
from jax import lax
from jax.sharding import PartitionSpec as P


def swapped(block, axis, bit):
    count = lax.axis_size(axis)
    route = []
    for low in range(count):
        high = low | 1 << bit
        if high != low and high < count:
            route += [(low, high), (high, low)]
    return lax.ppermute(block, axis, route)


def block_images(values, row_ids, col_ids, panel_rows, out_blocks):
    orbitals = values.shape[-1]
    vec_count = panel_rows.shape[-1]
    blocks = panel_rows.reshape(-1, orbitals, vec_count)
    block_count = values.shape[0]
    group_size = math.gcd(block_count, 64)

    def add_group(row_images, group_items):
        group_values, group_rows, group_cols = group_items
        picked = blocks[group_cols]
        images = jnp.einsum(
            "gij,gjv->giv", group_values, picked, preferred_element_type=jnp.float32
        )
        return (row_images.at[group_rows].add(images), None)

    initial = jnp.zeros((out_blocks, orbitals, vec_count), jnp.float32)
    turns = block_count // group_size
    group_items = (
        values.reshape(turns, group_size, orbitals, orbitals),
        row_ids.reshape(turns, group_size),
        col_ids.reshape(turns, group_size),
    )
    row_images, _ = lax.scan(add_group, initial, group_items)
    return row_images.reshape(out_blocks * orbitals, vec_count)


def on_device(block_values, block_rows, block_cols, start_vectors, center, half_width, row_counts):
    orbitals = block_values.shape[-1]
    values = block_values.reshape(-1, orbitals, orbitals)
    row_ids = block_rows.reshape(-1)
    col_ids = block_cols.reshape(-1)
    own_rows, vec_count = start_vectors.shape
    own_blocks = own_rows // orbitals
    col_count = lax.axis_size("col")
    center_value = center[0]
    width_value = half_width[0]

    def image_of(vectors):
        panel_rows = lax.all_gather(vectors, "row", axis=0, tiled=True)
        cell_terms = block_images(values, row_ids, col_ids, panel_rows, col_count * own_blocks)
        return lax.psum_scatter(
            cell_terms.astype(jnp.bfloat16), "col", scatter_dimension=0, tiled=True
        ).astype(jnp.float32)

    source = start_vectors.astype(jnp.float32)
    first_image = image_of(start_vectors)
    first_step = ((first_image - center_value * source) / width_value).astype(jnp.bfloat16)
    second_image = image_of(first_step)
    second = (
        2.0 * (second_image - center_value * first_step.astype(jnp.float32)) / width_value - source
    ).astype(jnp.bfloat16)
    device = lax.axis_index("row") * col_count + lax.axis_index("col")
    parity = device % 2
    even_count = row_counts[device - parity]
    own_count = row_counts[device]
    start_block = parity * even_count
    half_blocks = own_blocks // 2
    capacity = own_blocks + half_blocks
    partner = swapped(second, ("row", "col"), 0)
    window = jnp.where(
        parity == 0, jnp.concatenate([second, partner], 0), jnp.concatenate([partner, second], 0)
    )
    window_low = parity * 0
    padded = jnp.concatenate([window, jnp.zeros((capacity * orbitals, vec_count), jnp.bfloat16)], 0)
    selected = lax.dynamic_slice_in_dim(padded, start_block * orbitals, capacity * orbitals, 0)
    live_rows = jnp.arange(capacity * orbitals, dtype=jnp.int32)[:, None] < own_count * orbitals
    return jnp.where(live_rows, selected, jnp.zeros_like(selected))


def solution(mesh):
    placed = (
        P("row", "col", None, None, None),
        P("row", "col", None),
        P("row", "col", None),
        P(("row", "col"), None),
        P(),
        P(),
        P(),
    )
    return jax.shard_map(
        on_device, mesh=mesh, in_specs=placed, out_specs=P(("row", "col"), None), check_vma=False
    )
```

profile of v0, /device:TPU:0, one launch (start us, length us, event | category | flops | bytes accessed | tf_op | source)
XLA Modules:
  0.0 645.1 jit_solution(17980662493797626057)
XLA Ops:
  10.6 44.2 %all-gather.3.cloned.1.call-done = bf16[13312,256]{1,0:T(8,128)(2,1)} async-done(((bf16[1664,256]{1,0:T(8,128)(2,1)}), bf16[13312,256]{1,0:T(8,128)(2,1)}) %all-gather.3.cloned.1.call-update) | async-done | bytes 6815760 | tf_op jit(solution)/shard_map/all_gather | solution.py:56
  54.8 12.5 %broadcast.88.clone = f32[208,128,256]{2,1,0:T(8,128)} broadcast(f32[]{:T(128)} %constant.61.clone.1), dimensions={} | broadcast | bytes 27262980 | tf_op jit(solution)/shard_map/broadcast.15
  67.3 130.8 %while.20 = (s32[]{:T(128)}, f32[208,128,256]{2,1,0:T(8,128)}, s32[4,64]{1,0:T(4,128)S(1)}, bf16[4,64,128,128]{3,2,1,0:T(8,128)(2,1)}, s32[4,64]{1,0:T(4,128)S(1)}, /*index=5*/bf16[104,128,256]{2,1,0:T(8,128)(2,1)}, s32[]{:T(128)}) while((s32[]{:T(128)}, f32[208,128,256]{2,1,0:T(8,128)}, s32[4,64]{1,0:T(4,128)S(1)}, ...), condition=%wide.region_2.3_spmd, body=%wide.region_0.2_spmd.sunk | while | flops 538969472 | bytes 48240976 | solution.py:40
  80.3 19.6 %scatter_fusion = f32[208,128,256]{2,1,0:T(8,128)} fusion(f32[208,128,256]{2,1,0:T(8,128)} %get-tuple-element.191, s32[64]{0:T(128)S(1)} %get-tuple-element.173, f32[64,128,256]{2,1,0:T(8,128)} %fusion.35), kind=kCustom, calls=%fused_computation.2.clone.1 | custom fusion | flops 2097152 | bytes 25166080 | tf_op jit(solution)/shard_map/while/body/eval_jaxpr/scatter-add | solution.py:31
  105.6 7.3 %fusion.35 = f32[64,128,256]{2,1,0:T(8,128)} fusion(bf16[64,128,256]{2,1,0:T(8,128)(2,1)} %gather_fusion, bf16[4,64,128,128]{3,2,1,0:T(8,128)(2,1)} %get-tuple-element.200, s32[]{:T(128)} %get-tuple-element.190), kind=kOutput, calls=%fused_computation.4.clone.1 | convolution fusion | flops 536870912 | bytes 14680576 | tf_op jit(solution)/shard_map/while/body/eval_jaxpr/gij,gjv->giv/dot_general | solution.py:28
  112.9 19.7 %scatter_fusion = f32[208,128,256]{2,1,0:T(8,128)} fusion(f32[208,128,256]{2,1,0:T(8,128)} %get-tuple-element.191, s32[64]{0:T(128)S(1)} %get-tuple-element.173, f32[64,128,256]{2,1,0:T(8,128)} %fusion.35), kind=kCustom, calls=%fused_computation.2.clone.1 | custom fusion | flops 2097152 | bytes 25166080 | tf_op jit(solution)/shard_map/while/body/eval_jaxpr/scatter-add | solution.py:31
  138.4 7.3 %fusion.35 = f32[64,128,256]{2,1,0:T(8,128)} fusion(bf16[64,128,256]{2,1,0:T(8,128)(2,1)} %gather_fusion, bf16[4,64,128,128]{3,2,1,0:T(8,128)(2,1)} %get-tuple-element.200, s32[]{:T(128)} %get-tuple-element.190), kind=kOutput, calls=%fused_computation.4.clone.1 | convolution fusion | flops 536870912 | bytes 14680576 | tf_op jit(solution)/shard_map/while/body/eval_jaxpr/gij,gjv->giv/dot_general | solution.py:28
  145.7 19.8 %scatter_fusion = f32[208,128,256]{2,1,0:T(8,128)} fusion(f32[208,128,256]{2,1,0:T(8,128)} %get-tuple-element.191, s32[64]{0:T(128)S(1)} %get-tuple-element.173, f32[64,128,256]{2,1,0:T(8,128)} %fusion.35), kind=kCustom, calls=%fused_computation.2.clone.1 | custom fusion | flops 2097152 | bytes 25166080 | tf_op jit(solution)/shard_map/while/body/eval_jaxpr/scatter-add | solution.py:31
  171.2 7.3 %fusion.35 = f32[64,128,256]{2,1,0:T(8,128)} fusion(bf16[64,128,256]{2,1,0:T(8,128)(2,1)} %gather_fusion, bf16[4,64,128,128]{3,2,1,0:T(8,128)(2,1)} %get-tuple-element.200, s32[]{:T(128)} %get-tuple-element.190), kind=kOutput, calls=%fused_computation.4.clone.1 | convolution fusion | flops 536870912 | bytes 14680576 | tf_op jit(solution)/shard_map/while/body/eval_jaxpr/gij,gjv->giv/dot_general | solution.py:28
  178.5 19.6 %scatter_fusion = f32[208,128,256]{2,1,0:T(8,128)} fusion(f32[208,128,256]{2,1,0:T(8,128)} %get-tuple-element.191, s32[64]{0:T(128)S(1)} %get-tuple-element.173, f32[64,128,256]{2,1,0:T(8,128)} %fusion.35), kind=kCustom, calls=%fused_computation.2.clone.1 | custom fusion | flops 2097152 | bytes 25166080 | tf_op jit(solution)/shard_map/while/body/eval_jaxpr/scatter-add | solution.py:31
  198.1 15.5 %convert_element_type.30 = bf16[208,128,256]{2,1,0:T(8,128)(2,1)} convert(f32[208,128,256]{2,1,0:T(8,128)} %get-tuple-element.69) | non-fusion elementwise | flops 6815744 | bytes 40894464 | tf_op jit(solution)/shard_map/convert_element_type | solution.py:59
  215.1 96.4 %reduce-scatter.3.cloned.1.call-done = bf16[1664,256]{1,0:T(8,128)(2,1)} async-done(((bf16[26624,256]{1,0:T(8,128)(2,1)}), bf16[1664,256]{1,0:T(8,128)(2,1)}) %reduce-scatter.3.cloned.1.call-update) | async-done | bytes 851984 | tf_op jit(solution)/shard_map/reduce_scatter | solution.py:58
  313.9 42.2 %all-gather.5.cloned.1.call-done = bf16[13312,256]{1,0:T(8,128)(2,1)} async-done(((bf16[1664,256]{1,0:T(8,128)(2,1)}), bf16[13312,256]{1,0:T(8,128)(2,1)}) %all-gather.5.cloned.1.call-update) | async-done | bytes 6815760 | tf_op jit(solution)/shard_map/all_gather | solution.py:56
  356.1 12.5 %broadcast.88 = f32[208,128,256]{2,1,0:T(8,128)} broadcast(f32[]{:T(128)} %constant.61.clone.1), dimensions={} | broadcast | bytes 27262980 | tf_op jit(solution)/shard_map/broadcast.15
  368.5 130.8 %while.21 = (s32[]{:T(128)}, f32[208,128,256]{2,1,0:T(8,128)}, s32[4,64]{1,0:T(4,128)S(1)}, bf16[4,64,128,128]{3,2,1,0:T(8,128)(2,1)}, s32[4,64]{1,0:T(4,128)S(1)}, /*index=5*/bf16[104,128,256]{2,1,0:T(8,128)(2,1)}, s32[]{:T(128)}) while((s32[]{:T(128)}, f32[208,128,256]{2,1,0:T(8,128)}, s32[4,64]{1,0:T(4,128)S(1)}, ...), condition=%wide.region_6.7_spmd, body=%wide.region_4.6_spmd.sunk | while | flops 538969472 | bytes 48240976 | solution.py:40
  374.3 7.3 %fusion.39 = f32[64,128,256]{2,1,0:T(8,128)} fusion(bf16[64,128,256]{2,1,0:T(8,128)(2,1)} %gather_fusion.1, bf16[4,64,128,128]{3,2,1,0:T(8,128)(2,1)} %get-tuple-element.221, s32[]{:T(128)} %get-tuple-element.211), kind=kOutput, calls=%fused_computation.17.clone.1 | convolution fusion | flops 536870912 | bytes 14680576 | tf_op jit(solution)/shard_map/while/body/eval_jaxpr/gij,gjv->giv/dot_general | solution.py:28
  381.6 19.6 %scatter_fusion.1 = f32[208,128,256]{2,1,0:T(8,128)} fusion(f32[208,128,256]{2,1,0:T(8,128)} %get-tuple-element.212, s32[64]{0:T(128)S(1)} %get-tuple-element.181, f32[64,128,256]{2,1,0:T(8,128)} %fusion.39), kind=kCustom, calls=%fused_computation.3.clone.1 | custom fusion | flops 2097152 | bytes 25166080 | tf_op jit(solution)/shard_map/while/body/eval_jaxpr/scatter-add | solution.py:31
  414.2 19.7 %scatter_fusion.1 = f32[208,128,256]{2,1,0:T(8,128)} fusion(f32[208,128,256]{2,1,0:T(8,128)} %get-tuple-element.212, s32[64]{0:T(128)S(1)} %get-tuple-element.181, f32[64,128,256]{2,1,0:T(8,128)} %fusion.39), kind=kCustom, calls=%fused_computation.3.clone.1 | custom fusion | flops 2097152 | bytes 25166080 | tf_op jit(solution)/shard_map/while/body/eval_jaxpr/scatter-add | solution.py:31
  447.0 19.8 %scatter_fusion.1 = f32[208,128,256]{2,1,0:T(8,128)} fusion(f32[208,128,256]{2,1,0:T(8,128)} %get-tuple-element.212, s32[64]{0:T(128)S(1)} %get-tuple-element.181, f32[64,128,256]{2,1,0:T(8,128)} %fusion.39), kind=kCustom, calls=%fused_computation.3.clone.1 | custom fusion | flops 2097152 | bytes 25166080 | tf_op jit(solution)/shard_map/while/body/eval_jaxpr/scatter-add | solution.py:31
  472.5 7.3 %fusion.39 = f32[64,128,256]{2,1,0:T(8,128)} fusion(bf16[64,128,256]{2,1,0:T(8,128)(2,1)} %gather_fusion.1, bf16[4,64,128,128]{3,2,1,0:T(8,128)(2,1)} %get-tuple-element.221, s32[]{:T(128)} %get-tuple-element.211), kind=kOutput, calls=%fused_computation.17.clone.1 | convolution fusion | flops 536870912 | bytes 14680576 | tf_op jit(solution)/shard_map/while/body/eval_jaxpr/gij,gjv->giv/dot_general | solution.py:28
  479.8 19.6 %scatter_fusion.1 = f32[208,128,256]{2,1,0:T(8,128)} fusion(f32[208,128,256]{2,1,0:T(8,128)} %get-tuple-element.212, s32[64]{0:T(128)S(1)} %get-tuple-element.181, f32[64,128,256]{2,1,0:T(8,128)} %fusion.39), kind=kCustom, calls=%fused_computation.3.clone.1 | custom fusion | flops 2097152 | bytes 25166080 | tf_op jit(solution)/shard_map/while/body/eval_jaxpr/scatter-add | solution.py:31
  499.4 15.5 %convert_element_type.35 = bf16[208,128,256]{2,1,0:T(8,128)(2,1)} convert(f32[208,128,256]{2,1,0:T(8,128)} %get-tuple-element.70) | non-fusion elementwise | flops 6815744 | bytes 40894464 | tf_op jit(solution)/shard_map/convert_element_type | solution.py:59
  514.9 97.9 %reduce-scatter.5.cloned.1.call-done = bf16[1664,256]{1,0:T(8,128)(2,1)} async-done(((bf16[26624,256]{1,0:T(8,128)(2,1)}), bf16[1664,256]{1,0:T(8,128)(2,1)}) %reduce-scatter.5.cloned.1.call-update) | async-done | bytes 851984 | tf_op jit(solution)/shard_map/reduce_scatter | solution.py:58
  617.5 17.6 %collective-permute-done = bf16[1664,256]{1,0:T(8,128)(2,1)S(1)} collective-permute-done((bf16[1664,256]{1,0:T(8,128)(2,1)S(1)}, bf16[1664,256]{1,0:T(8,128)(2,1)S(1)}, u32[]{:S(2)}, u32[]{:S(2)}) %collective-permute-start) | collective-permute-done | bytes 852000 | tf_op jit(solution)/shard_map/ppermute | solution.py:15
  (53 shorter events, 81.2 us)
Async XLA Ops:
  6.5 48.3 %all-gather.3.cloned.1.call-start = ((), (), s32[]{:S(2)}) async-start(), calls=%async_computation.2 | async-start | bytes 7667712 | tf_op jit(solution)/shard_map/all_gather | solution.py:56
  7.3 304.2 %reduce-scatter.3.cloned.1.call-start = ((), (), s32[]{:S(2)}) async-start(), calls=%async_computation.3 | async-start | bytes 14483456 | tf_op jit(solution)/shard_map/reduce_scatter | solution.py:58
  213.6 97.9 %copy-start = (bf16[1664,256]{1,0:T(8,128)(2,1)S(1)}, bf16[1664,256]{1,0:T(8,128)(2,1)}, u32[]{:S(2)}) copy-start(bf16[1664,256]{1,0:T(8,128)(2,1)} %param.14) | copy-start | bytes 2555908
  213.7 142.4 %all-gather.5.cloned.1.call-start = ((), (), s32[]{:S(2)}) async-start(), calls=%async_computation.4 | async-start | bytes 7667712 | tf_op jit(solution)/shard_map/all_gather | solution.py:56
  313.9 298.9 %reduce-scatter.5.cloned.1.call-start = ((), (), s32[]{:S(2)}) async-start(), calls=%async_computation.5 | async-start | bytes 14483456 | tf_op jit(solution)/shard_map/reduce_scatter | solution.py:58
  514.9 97.9 %copy-start.1 = (bf16[1664,256]{1,0:T(8,128)(2,1)S(1)}, bf16[1664,256]{1,0:T(8,128)(2,1)}, u32[]{:S(2)}) copy-start(bf16[1664,256]{1,0:T(8,128)(2,1)} %reduce-scatter.3.cloned.1.call-done) | copy-start | bytes 2555908
  514.9 100.7 %copy-start.2 = (s32[128]{0:T(128)S(1)}, s32[128]{0:T(128)}, u32[]{:S(2)}) copy-start(s32[128]{0:T(128)} %param.17) | copy-start | bytes 1540
  614.7 20.4 %collective-permute-start = (bf16[1664,256]{1,0:T(8,128)(2,1)S(1)}, bf16[1664,256]{1,0:T(8,128)(2,1)S(1)}, u32[]{:S(2)}, u32[]{:S(2)}) collective-permute-start(bf16[1664,256]{1,0:T(8,128)(2,1)S(1)} %fusion.19), channel_id=1, source_target_pairs={{0,1},{1,0},{2,3},{3,2},{4,5},{5,4},{6,7},{7,6},{8,9},{9,8},{10,11... | collective-permute-start | bytes 2555912 | tf_op jit(solution)/shard_map/ppermute | solution.py:15
Sparse Core Ops, SparseCore 0:
  9.0 45.7 all-gather.2
  213.8 97.6 reduce-scatter.2
  314.0 42.0 all-gather.4
  515.1 97.6 reduce-scatter.4
where the time goes:
time: 646 us; the launch traced here: 645 us
  waiting for transfers between devices  299 us (46%)
  other arithmetic  199 us (31%)
  local copies, waits for them, and re-layouts  71.9 us (11%)
  matrix products  58.4 us (9%)
  between operations  15.8 us (2%)
    reduce_scatter x2, waiting for transfers between devices, image_of(): lax.psum_scatter(cell_terms.astype(jnp.bfloat16), 'col', scatter_dimensio...  194 us
    scatter-add x8, other arithmetic, add_group(): return (row_images.at[group_rows].add(images), None)  157 us
    all_gather x2, waiting for transfers between devices, image_of(): panel_rows = lax.all_gather(vectors, 'row', axis=0, tiled=True)  86.3 us
    dot_general x8, matrix products, add_group(): jnp.einsum('gij,gjv->giv', group_values, picked, preferred_element_type=j...  58.4 us
    gather x8, local copies, waits for them, and re-layouts, add_group(): picked = blocks[group_cols]  45.7 us
    convert_element_type x2, other arithmetic, image_of(): cell_terms.astype(jnp.bfloat16)  31.1 us
    another operation x2, local copies, waits for them, and re-layouts  24.9 us
    ppermute x1, waiting for transfers between devices, swapped(): return lax.ppermute(block, axis, route)  17.6 us
  transfers between devices with their start and end apart: 5, of which 5 were waited for; matrix products, arithmetic and copies ran while one was open for 1% of the time, Pallas kernels for 0%

commit v1 on v0

--- a/solution.py
+++ b/solution.py
@@ -53,7 +53,9 @@
     width_value = half_width[0]
 
     def image_of(vectors):
-        panel_rows = lax.all_gather(vectors, "row", axis=0, tiled=True)
+        panel_rows = jnp.concatenate(
+            lax.all_to_all(jnp.stack([vectors] * lax.axis_size("row")), "row", 0, 0), axis=0
+        )
         cell_terms = block_images(values, row_ids, col_ids, panel_rows, col_count * own_blocks)
         return lax.psum_scatter(
             cell_terms.astype(jnp.bfloat16), "col", scatter_dimension=0, tiled=True

time: 646 us -> 726 us (1.12)
  waiting for transfers between devices: 299 us -> 363 us
  starting transfers between devices: 1 us -> 11.5 us
  local copies, waits for them, and re-layouts: 71.9 us -> 79.5 us
    all_to_all x0 -> x2, waiting for transfers between devices: none -> 153 us  [image_of(): lax.all_to_all(jnp.stack([vectors] * lax.axis_size('row')), 'row', 0, 0)]
    all_gather x2 -> x0, waiting for transfers between devices: 86.3 us -> none  [image_of(): panel_rows = lax.all_gather(vectors, 'row', axis=0, tiled=True)]
    all_to_all x0 -> x2, starting transfers between devices: none -> 10.4 us  [image_of(): lax.all_to_all(jnp.stack([vectors] * lax.axis_size('row')), 'row', 0, 0)]
    another operation x2 -> x4, local copies, waits for them, and re-layouts: 24.9 us -> 32.5 us
  transfers between devices with their start and end apart: 5 -> 5, of which waited for: 5 -> 5; matrix products, arithmetic and copies ran while one was open for 1% -> 0% of each run, Pallas kernels for 0% -> 0%
where the time goes in v1:
time: 726 us; the launch traced here: 725 us
  waiting for transfers between devices  363 us (50%)
  other arithmetic  197 us (27%)
  local copies, waits for them, and re-layouts  79.5 us (11%)
  matrix products  58.4 us (8%)
  between operations  16.1 us (2%)
  starting transfers between devices  11.5 us (2%)
    reduce_scatter x2, waiting for transfers between devices, image_of(): lax.psum_scatter(cell_terms.astype(jnp.bfloat16), 'col', scatter_dimensio...  192 us
    scatter-add x8, other arithmetic, add_group(): return (row_images.at[group_rows].add(images), None)  157 us
    all_to_all x2, waiting for transfers between devices, image_of(): lax.all_to_all(jnp.stack([vectors] * lax.axis_size('row')), 'row', 0, 0)  153 us
    dot_general x8, matrix products, add_group(): jnp.einsum('gij,gjv->giv', group_values, picked, preferred_element_type=j...  58.4 us
    gather x8, local copies, waits for them, and re-layouts, add_group(): picked = blocks[group_cols]  45.7 us
    convert_element_type x2, other arithmetic, image_of(): cell_terms.astype(jnp.bfloat16)  31.1 us
    another operation x2, local copies, waits for them, and re-layouts  24.9 us
    ppermute x1, waiting for transfers between devices, swapped(): return lax.ppermute(block, axis, route)  17.6 us
  transfers between devices with their start and end apart: 5, of which 5 were waited for; matrix products, arithmetic and copies ran while one was open for 0% of the time, Pallas kernels for 0%

profile of v1, /device:TPU:0, one launch (start us, length us, event | category | flops | bytes accessed | tf_op | source)
XLA Modules:
  0.0 724.8 jit_solution(6373839568551871150)
XLA Ops:
  18.4 76.0 %all-to-all-done = bf16[8,1664,256]{2,1,0:T(8,128)(2,1)} async-done(((bf16[8,1664,256]{2,1,0:T(8,128)(2,1)}), bf16[8,1664,256]{2,1,0:T(8,128)(2,1)}, u32[]{:S(2)}, u32[]{:S(2)}) %all-to-all-start) | async-done | bytes 6815776 | tf_op jit(solution)/shard_map/all_to_all | solution.py:57
  94.3 12.5 %broadcast.92.clone = f32[208,128,256]{2,1,0:T(8,128)} broadcast(f32[]{:T(128)} %constant.61.clone.1), dimensions={} | broadcast | bytes 27262980 | tf_op jit(solution)/shard_map/broadcast.15
  106.8 130.8 %while.20 = (s32[]{:T(128)}, f32[208,128,256]{2,1,0:T(8,128)}, s32[4,64]{1,0:T(4,128)S(1)}, bf16[4,64,128,128]{3,2,1,0:T(8,128)(2,1)}, s32[4,64]{1,0:T(4,128)S(1)}, /*index=5*/bf16[104,128,256]{2,1,0:T(8,128)(2,1)}, s32[]{:T(128)}) while((s32[]{:T(128)}, f32[208,128,256]{2,1,0:T(8,128)}, s32[4,64]{1,0:T(4,128)S(1)}, ...), condition=%wide.region_2.3_spmd, body=%wide.region_0.2_spmd.sunk | while | flops 538969472 | bytes 48240976 | solution.py:40
  112.5 7.3 %fusion.35 = f32[64,128,256]{2,1,0:T(8,128)} fusion(bf16[64,128,256]{2,1,0:T(8,128)(2,1)} %gather_fusion, bf16[4,64,128,128]{3,2,1,0:T(8,128)(2,1)} %get-tuple-element.200, s32[]{:T(128)} %get-tuple-element.190), kind=kOutput, calls=%fused_computation.4.clone.1 | convolution fusion | flops 536870912 | bytes 14680576 | tf_op jit(solution)/shard_map/while/body/eval_jaxpr/gij,gjv->giv/dot_general | solution.py:28
  119.8 19.6 %scatter_fusion = f32[208,128,256]{2,1,0:T(8,128)} fusion(f32[208,128,256]{2,1,0:T(8,128)} %get-tuple-element.191, s32[64]{0:T(128)S(1)} %get-tuple-element.173, f32[64,128,256]{2,1,0:T(8,128)} %fusion.35), kind=kCustom, calls=%fused_computation.2.clone.1 | custom fusion | flops 2097152 | bytes 25166080 | tf_op jit(solution)/shard_map/while/body/eval_jaxpr/scatter-add | solution.py:31
  145.1 7.3 %fusion.35 = f32[64,128,256]{2,1,0:T(8,128)} fusion(bf16[64,128,256]{2,1,0:T(8,128)(2,1)} %gather_fusion, bf16[4,64,128,128]{3,2,1,0:T(8,128)(2,1)} %get-tuple-element.200, s32[]{:T(128)} %get-tuple-element.190), kind=kOutput, calls=%fused_computation.4.clone.1 | convolution fusion | flops 536870912 | bytes 14680576 | tf_op jit(solution)/shard_map/while/body/eval_jaxpr/gij,gjv->giv/dot_general | solution.py:28
  152.4 19.7 %scatter_fusion = f32[208,128,256]{2,1,0:T(8,128)} fusion(f32[208,128,256]{2,1,0:T(8,128)} %get-tuple-element.191, s32[64]{0:T(128)S(1)} %get-tuple-element.173, f32[64,128,256]{2,1,0:T(8,128)} %fusion.35), kind=kCustom, calls=%fused_computation.2.clone.1 | custom fusion | flops 2097152 | bytes 25166080 | tf_op jit(solution)/shard_map/while/body/eval_jaxpr/scatter-add | solution.py:31
  177.9 7.3 %fusion.35 = f32[64,128,256]{2,1,0:T(8,128)} fusion(bf16[64,128,256]{2,1,0:T(8,128)(2,1)} %gather_fusion, bf16[4,64,128,128]{3,2,1,0:T(8,128)(2,1)} %get-tuple-element.200, s32[]{:T(128)} %get-tuple-element.190), kind=kOutput, calls=%fused_computation.4.clone.1 | convolution fusion | flops 536870912 | bytes 14680576 | tf_op jit(solution)/shard_map/while/body/eval_jaxpr/gij,gjv->giv/dot_general | solution.py:28
  185.2 19.8 %scatter_fusion = f32[208,128,256]{2,1,0:T(8,128)} fusion(f32[208,128,256]{2,1,0:T(8,128)} %get-tuple-element.191, s32[64]{0:T(128)S(1)} %get-tuple-element.173, f32[64,128,256]{2,1,0:T(8,128)} %fusion.35), kind=kCustom, calls=%fused_computation.2.clone.1 | custom fusion | flops 2097152 | bytes 25166080 | tf_op jit(solution)/shard_map/while/body/eval_jaxpr/scatter-add | solution.py:31
  210.7 7.3 %fusion.35 = f32[64,128,256]{2,1,0:T(8,128)} fusion(bf16[64,128,256]{2,1,0:T(8,128)(2,1)} %gather_fusion, bf16[4,64,128,128]{3,2,1,0:T(8,128)(2,1)} %get-tuple-element.200, s32[]{:T(128)} %get-tuple-element.190), kind=kOutput, calls=%fused_computation.4.clone.1 | convolution fusion | flops 536870912 | bytes 14680576 | tf_op jit(solution)/shard_map/while/body/eval_jaxpr/gij,gjv->giv/dot_general | solution.py:28
  218.0 19.6 %scatter_fusion = f32[208,128,256]{2,1,0:T(8,128)} fusion(f32[208,128,256]{2,1,0:T(8,128)} %get-tuple-element.191, s32[64]{0:T(128)S(1)} %get-tuple-element.173, f32[64,128,256]{2,1,0:T(8,128)} %fusion.35), kind=kCustom, calls=%fused_computation.2.clone.1 | custom fusion | flops 2097152 | bytes 25166080 | tf_op jit(solution)/shard_map/while/body/eval_jaxpr/scatter-add | solution.py:31
  237.6 15.5 %convert_element_type.30 = bf16[208,128,256]{2,1,0:T(8,128)(2,1)} convert(f32[208,128,256]{2,1,0:T(8,128)} %get-tuple-element.69) | non-fusion elementwise | flops 6815744 | bytes 40894464 | tf_op jit(solution)/shard_map/convert_element_type | solution.py:61
  254.5 96.4 %reduce-scatter.3.cloned.1.call-done = bf16[1664,256]{1,0:T(8,128)(2,1)} async-done(((bf16[26624,256]{1,0:T(8,128)(2,1)}), bf16[1664,256]{1,0:T(8,128)(2,1)}) %reduce-scatter.3.cloned.1.call-update) | async-done | bytes 851984 | tf_op jit(solution)/shard_map/reduce_scatter | solution.py:60
  360.7 77.5 %all-to-all-done.1 = bf16[8,1664,256]{2,1,0:T(8,128)(2,1)} async-done(((bf16[8,1664,256]{2,1,0:T(8,128)(2,1)}), bf16[8,1664,256]{2,1,0:T(8,128)(2,1)}, u32[]{:S(2)}, u32[]{:S(2)}) %all-to-all-start.1) | async-done | bytes 6815776 | tf_op jit(solution)/shard_map/all_to_all | solution.py:57
  438.2 12.5 %broadcast.92 = f32[208,128,256]{2,1,0:T(8,128)} broadcast(f32[]{:T(128)} %constant.61.clone.1), dimensions={} | broadcast | bytes 27262980 | tf_op jit(solution)/shard_map/broadcast.15
  450.6 130.8 %while.21 = (s32[]{:T(128)}, f32[208,128,256]{2,1,0:T(8,128)}, s32[4,64]{1,0:T(4,128)S(1)}, bf16[4,64,128,128]{3,2,1,0:T(8,128)(2,1)}, s32[4,64]{1,0:T(4,128)S(1)}, /*index=5*/bf16[104,128,256]{2,1,0:T(8,128)(2,1)}, s32[]{:T(128)}) while((s32[]{:T(128)}, f32[208,128,256]{2,1,0:T(8,128)}, s32[4,64]{1,0:T(4,128)S(1)}, ...), condition=%wide.region_6.7_spmd, body=%wide.region_4.6_spmd.sunk | while | flops 538969472 | bytes 48240976 | solution.py:40
  463.6 19.6 %scatter_fusion.1 = f32[208,128,256]{2,1,0:T(8,128)} fusion(f32[208,128,256]{2,1,0:T(8,128)} %get-tuple-element.212, s32[64]{0:T(128)S(1)} %get-tuple-element.181, f32[64,128,256]{2,1,0:T(8,128)} %fusion.39), kind=kCustom, calls=%fused_computation.3.clone.1 | custom fusion | flops 2097152 | bytes 25166080 | tf_op jit(solution)/shard_map/while/body/eval_jaxpr/scatter-add | solution.py:31
  489.0 7.3 %fusion.39 = f32[64,128,256]{2,1,0:T(8,128)} fusion(bf16[64,128,256]{2,1,0:T(8,128)(2,1)} %gather_fusion.1, bf16[4,64,128,128]{3,2,1,0:T(8,128)(2,1)} %get-tuple-element.221, s32[]{:T(128)} %get-tuple-element.211), kind=kOutput, calls=%fused_computation.17.clone.1 | convolution fusion | flops 536870912 | bytes 14680576 | tf_op jit(solution)/shard_map/while/body/eval_jaxpr/gij,gjv->giv/dot_general | solution.py:28
  496.3 19.7 %scatter_fusion.1 = f32[208,128,256]{2,1,0:T(8,128)} fusion(f32[208,128,256]{2,1,0:T(8,128)} %get-tuple-element.212, s32[64]{0:T(128)S(1)} %get-tuple-element.181, f32[64,128,256]{2,1,0:T(8,128)} %fusion.39), kind=kCustom, calls=%fused_computation.3.clone.1 | custom fusion | flops 2097152 | bytes 25166080 | tf_op jit(solution)/shard_map/while/body/eval_jaxpr/scatter-add | solution.py:31
  529.0 19.8 %scatter_fusion.1 = f32[208,128,256]{2,1,0:T(8,128)} fusion(f32[208,128,256]{2,1,0:T(8,128)} %get-tuple-element.212, s32[64]{0:T(128)S(1)} %get-tuple-element.181, f32[64,128,256]{2,1,0:T(8,128)} %fusion.39), kind=kCustom, calls=%fused_computation.3.clone.1 | custom fusion | flops 2097152 | bytes 25166080 | tf_op jit(solution)/shard_map/while/body/eval_jaxpr/scatter-add | solution.py:31
  561.9 19.6 %scatter_fusion.1 = f32[208,128,256]{2,1,0:T(8,128)} fusion(f32[208,128,256]{2,1,0:T(8,128)} %get-tuple-element.212, s32[64]{0:T(128)S(1)} %get-tuple-element.181, f32[64,128,256]{2,1,0:T(8,128)} %fusion.39), kind=kCustom, calls=%fused_computation.3.clone.1 | custom fusion | flops 2097152 | bytes 25166080 | tf_op jit(solution)/shard_map/while/body/eval_jaxpr/scatter-add | solution.py:31
  581.5 15.5 %convert_element_type.35 = bf16[208,128,256]{2,1,0:T(8,128)(2,1)} convert(f32[208,128,256]{2,1,0:T(8,128)} %get-tuple-element.70) | non-fusion elementwise | flops 6815744 | bytes 40894464 | tf_op jit(solution)/shard_map/convert_element_type | solution.py:61
  597.0 95.2 %reduce-scatter.5.cloned.1.call-done = bf16[1664,256]{1,0:T(8,128)(2,1)} async-done(((bf16[26624,256]{1,0:T(8,128)(2,1)}), bf16[1664,256]{1,0:T(8,128)(2,1)}) %reduce-scatter.5.cloned.1.call-update) | async-done | bytes 851984 | tf_op jit(solution)/shard_map/reduce_scatter | solution.py:60
  696.8 17.6 %collective-permute-done = bf16[1664,256]{1,0:T(8,128)(2,1)S(1)} collective-permute-done((bf16[1664,256]{1,0:T(8,128)(2,1)S(1)}, bf16[1664,256]{1,0:T(8,128)(2,1)S(1)}, u32[]{:S(2)}, u32[]{:S(2)}) %collective-permute-start) | collective-permute-done | bytes 852000 | tf_op jit(solution)/shard_map/ppermute | solution.py:15
  (57 shorter events, 96.1 us)
Async XLA Ops:
  10.9 6.1 copy-start.3
  10.9 6.8 copy-start.4
  10.9 83.4 %all-to-all-start = ((bf16[8,1664,256]{2,1,0:T(8,128)(2,1)}), bf16[8,1664,256]{2,1,0:T(8,128)(2,1)}, u32[]{:S(2)}, u32[]{:S(2)}) async-start(bf16[8,1664,256]{2,1,0:T(8,128)(2,1)} %stack.4), calls=%async_computation | async-start | bytes 13631488 | tf_op jit(solution)/shard_map/all_to_all | solution.py:57
  16.5 334.5 %reduce-scatter.3.cloned.1.call-start = ((), (), s32[]{:S(2)}) async-start(), calls=%async_computation.4 | async-start | bytes 14483456 | tf_op jit(solution)/shard_map/reduce_scatter | solution.py:60
  253.1 97.8 %copy-start = (bf16[1664,256]{1,0:T(8,128)(2,1)S(1)}, bf16[1664,256]{1,0:T(8,128)(2,1)}, u32[]{:S(2)}) copy-start(bf16[1664,256]{1,0:T(8,128)(2,1)} %param.14) | copy-start | bytes 2555908
  355.6 82.5 %all-to-all-start.1 = ((bf16[8,1664,256]{2,1,0:T(8,128)(2,1)}), bf16[8,1664,256]{2,1,0:T(8,128)(2,1)}, u32[]{:S(2)}, u32[]{:S(2)}) async-start(bf16[8,1664,256]{2,1,0:T(8,128)(2,1)} %stack.5), calls=%async_computation.2 | async-start | bytes 13631488 | tf_op jit(solution)/shard_map/all_to_all | solution.py:57
  360.4 331.7 %reduce-scatter.5.cloned.1.call-start = ((), (), s32[]{:S(2)}) async-start(), calls=%async_computation.5 | async-start | bytes 14483456 | tf_op jit(solution)/shard_map/reduce_scatter | solution.py:60
  597.0 95.2 %copy-start.1 = (bf16[1664,256]{1,0:T(8,128)(2,1)S(1)}, bf16[1664,256]{1,0:T(8,128)(2,1)}, u32[]{:S(2)}) copy-start(bf16[1664,256]{1,0:T(8,128)(2,1)} %reduce-scatter.3.cloned.1.call-done) | copy-start | bytes 2555908
  597.0 98.0 %copy-start.2 = (s32[128]{0:T(128)S(1)}, s32[128]{0:T(128)}, u32[]{:S(2)}) copy-start(s32[128]{0:T(128)} %param.17) | copy-start | bytes 1540
  694.1 20.4 %collective-permute-start = (bf16[1664,256]{1,0:T(8,128)(2,1)S(1)}, bf16[1664,256]{1,0:T(8,128)(2,1)S(1)}, u32[]{:S(2)}, u32[]{:S(2)}) collective-permute-start(bf16[1664,256]{1,0:T(8,128)(2,1)S(1)} %fusion.19), channel_id=1, source_target_pairs={{0,1},{1,0},{2,3},{3,2},{4,5},{5,4},{6,7},{7,6},{8,9},{9,8},{10,11... | collective-permute-start | bytes 2555912 | tf_op jit(solution)/shard_map/ppermute | solution.py:15
Sparse Core Ops, SparseCore 0:
  253.3 97.5 reduce-scatter.2
  597.1 94.9 reduce-scatter.4
